TPU v7x, 32 devices: a whole 2x2x4 slice. The times are simulated.
32 devices in a mesh: groups: 2 (over x), chan: 16 (over z, y, core).
Axes of the slice: x: 2, y: 2, z: 4, core: 2. Of those that a mesh axis runs over, the one named last changes fastest.
Arguments:
- data: bfloat16 [28672, 4096], P(('groups', 'chan')), parts along dimension 0, as said below
- alive: int32 [8192], P(('groups', 'chan')), parts along dimension 0, may hold values 0 or 1
- sources: int32 [2, 16], replicated, may hold values from 0 to 4095, as said below
Outputs:
- correlations: bfloat16 [4, 16, 256, 4096], P('groups', None, None, 'chan'), parts along dimension 0
There are 2 independent parts, one for each index of `groups`. A program takes and returns all parts, laid end to end along the dimension named above; an argument that names none is the same for every part. Nothing has to cross between parts.
Inputs may be any that keep to these rules, and one draw needn't show every extreme that they name: `sources`: no channel number appears twice in the array, and channel 4096 - 1 is always one of them. `data`: samples have channel and time-block scales of their own.
All inputs are finite; a program needn't handle non-finite values. No bound on the sum of `alive` on one device may be relied on, other than what follows from the above.
Results may differ from a plain program's by a relative error of at most 0.0076.
Values may be sent and summed in bfloat16 or wider, within the bound.
No kernel may reach another device: no remote copies, remote signals or barrier semaphores. Data moves between devices by JAX's collectives and lax.ppermute only.
A program may use at most 128 MiB of HBM per device.

v0:
```python
import math
import jax
import jax.numpy as jnp
from jax import lax
from jax.sharding import PartitionSpec as P

SEGMENT_LENGTH = 512
NF = 128
LAGS = 256
SRC = 16
ROUNDS = 2
SEGMENT_TALLY = 28


def forward_table():
    times = jnp.arange(SEGMENT_LENGTH, dtype=jnp.int32)[:, None]
    bins = jnp.arange(NF, dtype=jnp.int32)[None, :] + 1
    angle = 2.0 * math.pi / SEGMENT_LENGTH * (bins * times % SEGMENT_LENGTH).astype(jnp.float32)
    table = jnp.concatenate([jnp.cos(angle), -jnp.sin(angle)], axis=1) / math.sqrt(SEGMENT_LENGTH)
    return table.astype(jnp.bfloat16)


def inverse_table():
    shifts = jnp.arange(LAGS, dtype=jnp.int32)[:, None] - LAGS // 2
    bins = jnp.arange(NF, dtype=jnp.int32)[None, :] + 1
    angle = 2.0 * math.pi / SEGMENT_LENGTH * (bins * shifts % SEGMENT_LENGTH).astype(jnp.float32)
    return jnp.concatenate([jnp.cos(angle), -jnp.sin(angle)], axis=1).astype(jnp.bfloat16)


def body(data, alive, sources):
    count = lax.axis_size("chan")
    width = data.shape[1] // count
    table = forward_table()
    split = data.reshape(data.shape[0], count, width)
    moved = lax.all_to_all(split, "chan", split_axis=1, concat_axis=0, tiled=True)
    blocks = moved.reshape(SEGMENT_TALLY, SEGMENT_LENGTH, moved.shape[2])
    spectra = jnp.einsum("tk,wtc->wkc", table, blocks, preferred_element_type=jnp.float32)
    level = jnp.mean(spectra[:, :NF] ** 2 + spectra[:, NF:] ** 2, axis=0)
    factor = alive.astype(jnp.float32)[None, :] / jnp.sqrt(level + 0.01)
    factor = jnp.concatenate([factor, factor], axis=0)
    whitened = (spectra * factor[None]).astype(jnp.bfloat16)
    ids = sources.reshape(-1)
    owner = ids // width
    local = ids % width
    mine = owner == lax.axis_index("chan")
    picked = jnp.transpose(jnp.take(whitened, local, axis=2), (2, 0, 1)).astype(jnp.float32)
    picked = jnp.where(mine[:, None, None], picked, 0.0)
    src = lax.psum(picked, "chan").astype(jnp.bfloat16)
    src_re, src_im = (src[:, :, :NF], src[:, :, NF:])
    own_re, own_im = (whitened[:, :NF], whitened[:, NF:])
    form = "qwf,wfc->qfc"
    correlogram_realpart = jnp.einsum(
        form, src_re, own_re, preferred_element_type=jnp.float32
    ) + jnp.einsum(form, src_im, own_im, preferred_element_type=jnp.float32)
    cross_imaginary = jnp.einsum(
        form, src_re, own_im, preferred_element_type=jnp.float32
    ) - jnp.einsum(form, src_im, own_re, preferred_element_type=jnp.float32)
    cross = jnp.concatenate([correlogram_realpart, cross_imaginary], axis=1).astype(jnp.bfloat16)
    lagged = jnp.einsum("lk,qkc->qlc", inverse_table(), cross, preferred_element_type=jnp.float32)
    lagged = lagged / math.sqrt(NF * SEGMENT_TALLY)
    return lagged.reshape(ROUNDS, SRC, LAGS, width).astype(jnp.bfloat16)


def solution(mesh):
    return jax.shard_map(
        body,
        mesh=mesh,
        in_specs=(P(("groups", "chan"), None), P(("groups", "chan")), P()),
        out_specs=P("groups", None, None, "chan"),
        check_vma=False,
    )
```

profile of v0, /device:TPU:0, one launch (start us, length us, event | category | flops | bytes accessed | tf_op | source)
XLA Modules:
  0.0 326.9 jit_solution(7985542122648060904)
XLA Ops:
  0.0 6.9 %copy.27 = bf16[112,16,8,256]{3,2,0,1:T(8,128)(2,1)} copy(bf16[112,16,8,256]{3,2,1,0:T(8,128)(2,1)} %bitcast.32) | data formatting | bytes 14680064 | tf_op jit(solution)/shard_map/reshape | solution.py:34
  6.9 7.6 %all-to-all-start = ((bf16[896,16,256]{2,0,1:T(8,128)(2,1)}), bf16[896,16,256]{2,0,1:T(8,128)(2,1)}, u32[]{:S(2)}, u32[]{:S(2)}) async-start(bf16[896,16,256]{2,0,1:T(8,128)(2,1)} %bitcast.31), calls=%async_computation | async-start | bytes 14680064 | tf_op jit(solution)/shard_map/all_to_all | solution.py:35
  14.4 0.0 copy-done.3
  14.4 0.1 reshape.125
  14.5 0.1 reshape.124
  14.6 0.0 copy-done.2
  14.7 0.6 cosine_convert_fusion
  15.3 1.1 fusion.33
  16.4 130.5 %all-to-all-done = bf16[896,16,256]{2,0,1:T(8,128)(2,1)} async-done(((bf16[896,16,256]{2,0,1:T(8,128)(2,1)}), bf16[896,16,256]{2,0,1:T(8,128)(2,1)}, u32[]{:S(2)}, u32[]{:S(2)}) %all-to-all-start) | async-done | bytes 7340064 | tf_op jit(solution)/shard_map/all_to_all | solution.py:35
  146.9 5.2 %convolution_bitcast_fusion = f32[28,256,256]{2,1,0:T(8,128)S(1)} fusion(bf16[28,512,256]{2,1,0:T(8,128)(2,1)} %bitcast.3, f32[512,128]{0,1:T(8,128)S(1)} %get-tuple-element.14, f32[512,128]{0,1:T(8,128)S(1)} %get-tuple-element.13), kind=kOutput, calls=%fused_computation.14 | convolution fusion | flops 1879441408 | bytes 15204352 | tf_op jit(solution)/shard_map/tk,wtc->wkc/dot_general | solution.py:37
  152.0 0.5 fusion.5
  152.6 2.6 multiply_convert_fusion.1
  155.2 7.7 %copy.7 = bf16[28,256,256]{1,0,2:T(8,128)(2,1)} copy(bf16[28,256,256]{2,1,0:T(8,128)(2,1)} %multiply_convert_fusion.1) | data formatting | bytes 7340032 | tf_op jit(solution)/shard_map/convert_element_type | solution.py:41
  162.9 3.6 %fusion.40 = (bf16[28,128,256]{2,1,0:T(8,128)(2,1)S(1)}, bf16[28,128,256]{2,1,0:T(8,128)(2,1)}) fusion(bf16[28,256,256]{2,1,0:T(8,128)(2,1)} %multiply_convert_fusion.1), kind=kLoop, calls=%fused_computation.76 | loop fusion | bytes 7340032 | tf_op jit(solution)/shard_map/slice | solution.py:50
  166.6 2.8 gather_fusion
  169.3 0.2 convert_select_fusion
  169.6 100.6 %all-reduce.1 = bf16[32,28,256]{2,1,0:T(8,128)(2,1)S(1)} all-reduce(f32[32,28,256]{2,1,0:T(8,128)S(1)} %convert_select_fusion), channel_id=1, replica_groups=mesh['groups'=2,'chan'=16] {'chan'}, use_global_device_ids=true, to_apply=%region_1.2 | all-reduce | flops 229376 | bytes 1376256 | tf_op jit(solution)/shard_map/psum | solution.py:48
  270.2 0.1 fusion.41
  270.3 2.6 copy.13
  272.8 1.6 copy.10
  274.5 0.0 copy-start.1
  274.5 4.6 %fusion.14 = f32[128,256,32]{1,2,0:T(8,128)} fusion(bf16[32,28,128]{0,1,2:T(8,128)(2,1)} %copy.13, bf16[28,128,256]{2,1,0:T(8,128)(2,1)S(1)} %get-tuple-element.5), kind=kOutput, calls=%fused_computation.21 | convolution fusion | flops 58720256 | bytes 6258688 | tf_op jit(solution)/shard_map/qwf,wfc->qfc/dot_general | solution.py:57
  279.1 3.2 fusion.12
  282.4 3.3 fusion.10
  285.6 3.3 %fusion.16 = f32[128,256,32]{1,2,0:T(8,128)} fusion(bf16[32,28,128]{0,1,2:T(8,128)(2,1)S(1)} %copy.10, bf16[28,128,256]{2,1,0:T(8,128)(2,1)S(1)} %get-tuple-element.5), kind=kOutput, calls=%fused_computation.23 | convolution fusion | flops 58720256 | bytes 6258688 | tf_op jit(solution)/shard_map/qwf,wfc->qfc/dot_general | solution.py:52
  288.9 5.3 %copy.16 = f32[128,256,32]{0,1,2:T(8,128)} copy(f32[128,256,32]{1,2,0:T(8,128)} %fusion.14) | data formatting | bytes 8388608 | tf_op jit(solution)/shard_map/qwf,wfc->qfc/dot_general | solution.py:57
  294.2 5.3 %copy.15 = f32[128,256,32]{0,1,2:T(8,128)} copy(f32[128,256,32]{1,2,0:T(8,128)} %fusion.10) | data formatting | bytes 8388608 | tf_op jit(solution)/shard_map/qwf,wfc->qfc/dot_general | solution.py:55
  299.6 5.3 %copy.14 = f32[128,256,32]{0,1,2:T(8,128)} copy(f32[128,256,32]{1,2,0:T(8,128)} %fusion.12) | data formatting | bytes 8388608 | tf_op jit(solution)/shard_map/qwf,wfc->qfc/dot_general | solution.py:54
  304.9 5.3 %copy.11 = f32[128,256,32]{0,1,2:T(8,128)} copy(f32[128,256,32]{1,2,0:T(8,128)} %fusion.16) | data formatting | bytes 8388608 | tf_op jit(solution)/shard_map/qwf,wfc->qfc/dot_general | solution.py:52
  310.2 7.6 %fusion.8 = (bf16[32,128,256]{1,2,0:T(8,128)(2,1)S(1)}, bf16[32,128,256]{1,2,0:T(8,128)(2,1)S(1)}) fusion(f32[128,256,32]{0,1,2:T(8,128)} %copy.11, f32[128,256,32]{0,1,2:T(8,128)} %copy.14, f32[128,256,32]{0,1,2:T(8,128)} %copy.15, f32[128,256,32]{0,1,2:T(8,128)} %copy.16), kind=kLoop, calls=%fused_computation.15 | loop fusion | flops 4194304 | bytes 20971520 | tf_op jit(solution)/shard_map/add | solution.py:52
  317.8 2.9 multiply_convert_fusion
  320.7 6.2 %copy.8 = bf16[2,16,256,256]{3,2,1,0:T(8,128)(2,1)} copy(bf16[2,16,256,256]{2,3,1,0:T(8,128)(2,1)} %bitcast.33) | data formatting | bytes 8388608 | tf_op jit(solution)/shard_map/convert_element_type | solution.py:61
  (13 shorter events, 0.1 us)
Async XLA Ops:
  6.9 7.6 %copy-start.3 = (s32[2,16]{1,0:T(2,128)S(1)}, s32[2,16]{1,0:T(2,128)}, u32[]{:S(2)}) copy-start(s32[2,16]{1,0:T(2,128)} %param.5) | copy-start | bytes 388
  6.9 7.8 %copy-start.2 = (s32[256]{0:T(256)S(1)}, s32[256]{0:T(256)}, u32[]{:S(2)}) copy-start(s32[256]{0:T(256)} %param.4) | copy-start | bytes 3076
  6.9 140.0 %all-to-all-start = ((bf16[896,16,256]{2,0,1:T(8,128)(2,1)}), bf16[896,16,256]{2,0,1:T(8,128)(2,1)}, u32[]{:S(2)}, u32[]{:S(2)}) async-start(bf16[896,16,256]{2,0,1:T(8,128)(2,1)} %bitcast.31), calls=%async_computation | async-start | bytes 14680064 | tf_op jit(solution)/shard_map/all_to_all | solution.py:35
  274.5 4.7 %copy-start = (bf16[28,128,256]{2,1,0:T(8,128)(2,1)S(1)}, bf16[28,128,256]{2,1,0:T(8,128)(2,1)}, u32[]{:S(2)}) copy-start(bf16[28,128,256]{2,1,0:T(8,128)(2,1)} %get-tuple-element.6) | copy-start | bytes 5505028
  274.5 4.7 %copy-start.1 = (bf16[32,28,128]{0,1,2:T(8,128)(2,1)S(1)}, bf16[32,28,128]{0,1,2:T(8,128)(2,1)}, u32[]{:S(2)}) copy-start(bf16[32,28,128]{0,1,2:T(8,128)(2,1)} %copy.13) | copy-start | bytes 688132
where the time goes:
time: 328 us; the launch traced here: 327 us
  waiting for transfers between devices  130 us (40%)
  blocking collectives  101 us (31%)
  local copies, waits for them, and re-layouts  52.9 us (16%)
  matrix products  22.5 us (7%)
  other arithmetic  12.8 us (4%)
  starting transfers between devices  7.56 us (2%)
    all_to_all x1, waiting for transfers between devices, body(): lax.all_to_all(split, 'chan', split_axis=1, concat_axis=0, tiled=True)  130 us
    psum x1, blocking collectives, body(): src = lax.psum(picked, 'chan').astype(jnp.bfloat16)  101 us
    convert_element_type x1, local copies, waits for them, and re-layouts, body(): whitened = (spectra * factor[None]).astype(jnp.bfloat16)  7.7 us
    add x1, other arithmetic, body(): jnp.einsum(form, src_re, own_re, preferred_element_type=jnp.float32)  7.63 us
    all_to_all x1, starting transfers between devices, body(): lax.all_to_all(split, 'chan', split_axis=1, concat_axis=0, tiled=True)  7.56 us
    reshape x1, local copies, waits for them, and re-layouts, body(): split = data.reshape(data.shape[0], count, width)  6.85 us
  transfers between devices with their start and end apart: 1, of which 1 were waited for; matrix products, arithmetic and copies ran while one was open for 1% of the time, Pallas kernels for 0%

commit v1 on v0

--- a/solution.py
+++ b/solution.py
@@ -10,6 +10,17 @@
 SRC = 16
 ROUNDS = 2
 SEGMENT_TALLY = 28
+
+
+def in_blocks(x, dim, devices):
+    before, after = (x.shape[:dim], x.shape[dim + 1 :])
+    return jnp.moveaxis(x.reshape(*before, devices, -1, *after), dim, 0)
+
+
+def laid_out(blocks, dim):
+    blocks = jnp.moveaxis(blocks, 0, dim)
+    lengths = blocks.shape
+    return blocks.reshape(*lengths[:dim], lengths[dim] * lengths[dim + 1], *lengths[dim + 2 :])
 
 
 def forward_table():
@@ -32,7 +43,15 @@
     width = data.shape[1] // count
     table = forward_table()
     split = data.reshape(data.shape[0], count, width)
-    moved = lax.all_to_all(split, "chan", split_axis=1, concat_axis=0, tiled=True)
+    count_2, mine_2 = (lax.axis_size("chan"), lax.axis_index("chan"))
+    pieces = in_blocks(split, 1, count_2)
+    out = pieces
+    for step in range(1, count_2):
+        target, source = ((mine_2 + step) % count_2, (mine_2 - step) % count_2)
+        sent = lax.dynamic_index_in_dim(pieces, target, 0)
+        other = lax.ppermute(sent, "chan", [(i, (i + step) % count_2) for i in range(count_2)])
+        out = lax.dynamic_update_slice_in_dim(out, other, source, axis=0)
+    moved = laid_out(out, 0)
     blocks = moved.reshape(SEGMENT_TALLY, SEGMENT_LENGTH, moved.shape[2])
     spectra = jnp.einsum("tk,wtc->wkc", table, blocks, preferred_element_type=jnp.float32)
     level = jnp.mean(spectra[:, :NF] ** 2 + spectra[:, NF:] ** 2, axis=0)

time: 328 us -> 351 us (1.070)
  starting transfers between devices: 7.56 us -> 81.6 us
  waiting for transfers between devices: 130 us -> 76.4 us
  local copies, waits for them, and re-layouts: 52.9 us -> 69.4 us
  other arithmetic: 12.8 us -> 6.3 us
  matrix products: 22.5 us -> 16.9 us
  blocking collectives: 101 us -> 96.2 us
    all_to_all x1 -> x0, waiting for transfers between devices: 130 us -> none  [body(): lax.all_to_all(split, 'chan', split_axis=1, concat_axis=0, tiled=True)]
    ppermute x0 -> x15, starting transfers between devices: none -> 81.6 us  [body(): lax.ppermute(sent, 'chan', [(i, (i + step) % count_2) for i in range(coun...]
    ppermute x0 -> x15, waiting for transfers between devices: none -> 76.4 us  [body(): lax.ppermute(sent, 'chan', [(i, (i + step) % count_2) for i in range(coun...]
    dynamic_update_slice x0 -> x16, local copies, waits for them, and re-layouts: none -> 23.4 us  [body(): out = lax.dynamic_update_slice_in_dim(out, other, source, axis=0)]
    dot_general x4 -> x0, local copies, waits for them, and re-layouts: 21.3 us -> none  [the longest x1 5.34 us: body(): jnp.einsum(form, src_re, own_im, preferred_element_type=jnp.float32)]
    unnamed x8 -> x17, local copies, waits for them, and re-layouts: 0.02 us -> 11.7 us
    slice x1 -> x3, local copies, waits for them, and re-layouts: 3.64 us -> 11.8 us  [body(): own_re, own_im = (whitened[:, :NF], whitened[:, NF:])]
    add x1 -> x0, other arithmetic: 7.63 us -> none  [body(): jnp.einsum(form, src_re, own_re, preferred_element_type=jnp.float32)]
  transfers between devices with their start and end apart: 1 -> 15, of which waited for: 1 -> 5; matrix products, arithmetic and copies ran while one was open for 1% -> 4% of each run, Pallas kernels for 0% -> 0%
where the time goes in v1:
time: 351 us; the launch traced here: 347 us
  blocking collectives  96.2 us (27%)
  starting transfers between devices  81.6 us (23%)
  waiting for transfers between devices  76.4 us (22%)
  local copies, waits for them, and re-layouts  69.4 us (20%)
  matrix products  16.9 us (5%)
  other arithmetic  6.3 us (2%)
    psum x1, blocking collectives, body(): src = lax.psum(picked, 'chan').astype(jnp.bfloat16)  96.2 us
    ppermute x15, starting transfers between devices, body(): lax.ppermute(sent, 'chan', [(i, (i + step) % count_2) for i in range(coun...  81.6 us
    ppermute x15, waiting for transfers between devices, body(): lax.ppermute(sent, 'chan', [(i, (i + step) % count_2) for i in range(coun...  76.4 us
    dynamic_update_slice x16, local copies, waits for them, and re-layouts, body(): out = lax.dynamic_update_slice_in_dim(out, other, source, axis=0)  23.4 us
    slice x3, local copies, waits for them, and re-layouts, body(): own_re, own_im = (whitened[:, :NF], whitened[:, NF:])  11.8 us
    unnamed x17, local copies, waits for them, and re-layouts  11.7 us
    dot_general x1, matrix products, body(): jnp.einsum('lk,qkc->qlc', inverse_table(), cross, preferred_element_type=...  7.24 us
  transfers between devices with their start and end apart: 15, of which 5 were waited for; matrix products, arithmetic and copies ran while one was open for 4% of the time, Pallas kernels for 0%

profile of v1, /device:TPU:0, one launch (start us, length us, event | category | flops | bytes accessed | tf_op | source)
XLA Modules:
  0.0 347.4 jit_solution(12167967714740710702)
XLA Ops:
  0.0 10.8 %copy.8 = bf16[896,4096]{0,1:T(8,128)(2,1)} copy(bf16[896,4096]{1,0:T(8,128)(2,1)} %param.3) | data formatting | bytes 14680064 | tf_op args[0]
  10.8 5.7 %dynamic-slice_bitcast_fusion = (bf16[1,896,1,256]{1,3,0,2:T(8,128)(2,1)S(1)}, bf16[1,896,1,256]{1,3,0,2:T(8,128)(2,1)}, bf16[1,896,1,256]{1,3,0,2:T(8,128)(2,1)...) fusion(bf16[896,16,1,256]{0,3,1,2:T(8,128)(2,1)} %bitcast.56, ...), kind=kLoop, calls=%fused_computation.24 | loop fusion | bytes 13762620 | tf_op jit(solution)/shard_map/jit(dynamic_index_in_dim)/dynamic_slice | solution.py:51
  17.0 2.6 collective-permute-start.1
  19.6 2.4 collective-permute-start.2
  22.0 1.6 collective-permute-start.3
  23.8 1.1 fusion.29
  26.0 6.4 %collective-permute-done = bf16[1,896,1,256]{1,3,0,2:T(8,128)(2,1)S(1)} collective-permute-done((bf16[1,896,1,256]{1,3,0,2:T(8,128)(2,1)}, bf16[1,896,1,256]{1,3,0,2:T(8,128)(2,1)S(1)}, u32[]{:S(2)}, u32[]{:S(2)}) %collective-permute-start) | collective-permute-done | bytes 458784 | tf_op jit(solution)/shard_map/ppermute | solution.py:52
  34.3 9.2 %collective-permute-start.6 = (bf16[1,896,1,256]{1,3,0,2:T(8,128)(2,1)}, bf16[1,896,1,256]{1,3,0,2:T(8,128)(2,1)S(1)}, u32[]{:S(2)}, u32[]{:S(2)}) collective-permute-start(bf16[1,896,1,256]{1,3,0,2:T(8,128)(2,1)} %get-tuple-element.13), channel_id=1, source_target_pairs={{0,7},{1,8},{2,9},{3,10},{4,11},{5,12},{6,13},{7,14},{8,15},{9,0},... | collective-permute-start | bytes 1376264 | tf_op jit(solution)/shard_map/ppermute | solution.py:52
  44.3 1.7 collective-permute-start.7
  47.8 64.0 %collective-permute-done.4 = bf16[1,896,1,256]{1,3,0,2:T(8,128)(2,1)S(1)} collective-permute-done((bf16[1,896,1,256]{1,3,0,2:T(8,128)(2,1)}, bf16[1,896,1,256]{1,3,0,2:T(8,128)(2,1)S(1)}, u32[]{:S(2)}, u32[]{:S(2)}) %collective-permute-start.4) | collective-permute-done | bytes 458784 | tf_op jit(solution)/shard_map/ppermute | solution.py:52
  112.7 11.4 %collective-permute-start.10 = (bf16[1,896,1,256]{1,3,0,2:T(8,128)(2,1)S(1)}, bf16[1,896,1,256]{1,3,0,2:T(8,128)(2,1)S(1)}, u32[]{:S(2)}, u32[]{:S(2)}) collective-permute-start(bf16[1,896,1,256]{1,3,0,2:T(8,128)(2,1)S(1)} %copy-done.5), channel_id=1, source_target_pairs={{0,11},{1,12},{2,13},{3,14},{4,15},{5,0},{6,1},{7,2},{8,3},{9,4},{... | collective-permute-start | bytes 1376264 | tf_op jit(solution)/shard_map/ppermute | solution.py:52
  124.9 23.1 %collective-permute-start.11 = (bf16[1,896,1,256]{1,3,0,2:T(8,128)(2,1)S(1)}, bf16[1,896,1,256]{1,3,0,2:T(8,128)(2,1)S(1)}, u32[]{:S(2)}, u32[]{:S(2)}) collective-permute-start(bf16[1,896,1,256]{1,3,0,2:T(8,128)(2,1)S(1)} %copy-done.4), channel_id=1, source_target_pairs={{0,12},{1,13},{2,14},{3,15},{4,0},{5,1},{6,2},{7,3},{8,4},{9,5},{1... | collective-permute-start | bytes 1376264 | tf_op jit(solution)/shard_map/ppermute | solution.py:52
  150.1 14.5 %collective-permute-start.13 = (bf16[1,896,1,256]{1,3,0,2:T(8,128)(2,1)S(1)}, bf16[1,896,1,256]{1,3,0,2:T(8,128)(2,1)S(1)}, u32[]{:S(2)}, u32[]{:S(2)}) collective-permute-start(bf16[1,896,1,256]{1,3,0,2:T(8,128)(2,1)S(1)} %copy-done.2), channel_id=1, source_target_pairs={{0,14},{1,15},{2,0},{3,1},{4,2},{5,3},{6,4},{7,5},{8,6},{9,7},{10,... | collective-permute-start | bytes 1376264 | tf_op jit(solution)/shard_map/ppermute | solution.py:52
  165.4 13.3 %collective-permute-start.14 = (bf16[1,896,1,256]{1,3,0,2:T(8,128)(2,1)S(1)}, bf16[1,896,1,256]{1,3,0,2:T(8,128)(2,1)S(1)}, u32[]{:S(2)}, u32[]{:S(2)}) collective-permute-start(bf16[1,896,1,256]{1,3,0,2:T(8,128)(2,1)S(1)} %get-tuple-element.5), channel_id=1, source_target_pairs={{0,15},{1,0},{2,1},{3,2},{4,3},{5,4},{6,5},{7,6},{8,7},{9,8},{10,9... | collective-permute-start | bytes 1376264 | tf_op jit(solution)/shard_map/ppermute | solution.py:52
  182.0 2.9 collective-permute-done.13
  184.9 0.8 constant_dynamic-update-slice_fusion.1
  185.8 2.5 collective-permute-done.14
  189.1 11.2 %copy.9 = bf16[16,896,1,256]{3,1,0,2:T(8,128)(2,1)} copy(bf16[16,896,1,256]{1,3,0,2:T(8,128)(2,1)} %constant_dynamic-update-slice_fusion) | data formatting | bytes 14680064 | tf_op jit(solution)/shard_map/dynamic_update_slice | solution.py:53
  200.3 5.2 %convolution_bitcast_fusion = f32[28,256,256]{1,2,0:T(8,128)S(1)} fusion(bf16[28,512,256]{2,1,0:T(8,128)(2,1)} %bitcast.58, f32[512,128]{1,0:T(8,128)S(1)} %get-tuple-element.27, f32[512,128]{1,0:T(8,128)S(1)} %get-tuple-element.26), kind=kOutput, calls=%fused_computation.13 | convolution fusion | flops 1879441408 | bytes 15204352 | tf_op jit(solution)/shard_map/tk,wtc->wkc/dot_general | solution.py:56
  206.1 1.0 multiply_convert_fusion.1
  207.1 4.2 %copy.11 = bf16[28,256,256]{1,0,2:T(8,128)(2,1)} copy(bf16[28,256,256]{1,2,0:T(8,128)(2,1)S(1)} %multiply_convert_fusion.1) | data formatting | bytes 7340032 | tf_op jit(solution)/shard_map/convert_element_type | solution.py:60
  211.3 2.9 fusion.36
  214.2 2.8 gather_fusion
  216.9 3.4 copy.12
  220.4 2.7 convert_select_fusion
  223.1 96.2 %all-reduce.1 = bf16[32,28,256]{1,0,2:T(8,128)(2,1)S(1)} all-reduce(f32[32,28,256]{1,0,2:T(8,128)} %convert_select_fusion), channel_id=1, replica_groups=mesh['groups'=2,'chan'=16] {'chan'}, use_global_device_ids=true, to_apply=%region_1.2 | all-reduce | flops 229376 | bytes 1376256 | tf_op jit(solution)/shard_map/psum | solution.py:67
  319.2 4.5 %copy.13 = bf16[28,128,256]{2,0,1:T(8,128)(2,1)} copy(bf16[28,128,256]{1,2,0:T(8,128)(2,1)} %get-tuple-element.20) | data formatting | bytes 3670016 | tf_op jit(solution)/shard_map/slice | solution.py:69
  323.8 4.4 %copy.14 = bf16[28,128,256]{2,0,1:T(8,128)(2,1)} copy(bf16[28,128,256]{1,2,0:T(8,128)(2,1)} %get-tuple-element.21) | data formatting | bytes 3670016 | tf_op jit(solution)/shard_map/slice | solution.py:69
  328.2 2.4 fusion.12
  332.0 0.9 copy-done
  334.0 7.2 %multiply_convert_fusion = bf16[32,256,256]{2,1,0:T(8,128)(2,1)} fusion(bf16[32,256,256]{2,0,1:T(8,128)(2,1)S(1)} %pad_maximum_fusion, bf16[256,128]{1,0:T(8,128)(2,1)S(1)} %get-tuple-element.23, bf16[256,128]{1,0:T(8,128)(2,1)S(1)} %get-tuple-element.22), kind=kOutput, calls=%fused_computation.1 | convolution fusion | flops 1078198272 | bytes 8519680 | tf_op jit(solution)/shard_map/lk,qkc->qlc/dot_general | solution.py:78
  341.2 6.2 %copy.18 = bf16[2,16,256,256]{3,2,1,0:T(8,128)(2,1)} copy(bf16[2,16,256,256]{2,3,1,0:T(8,128)(2,1)} %bitcast.59) | data formatting | bytes 8388608 | tf_op jit(solution)/shard_map/convert_element_type | solution.py:80
  (62 shorter events, 17.6 us)
Async XLA Ops:
  10.8 14.0 %copy-start.7 = (s32[2,16]{1,0:T(2,128)S(1)}, s32[2,16]{1,0:T(2,128)}, u32[]{:S(2)}) copy-start(s32[2,16]{1,0:T(2,128)} %param.5) | copy-start | bytes 388
  10.8 15.1 %copy-start.6 = (s32[256]{0:T(256)S(1)}, s32[256]{0:T(256)}, u32[]{:S(2)}) copy-start(s32[256]{0:T(256)} %param.4) | copy-start | bytes 3076
  16.5 16.0 %collective-permute-start = (bf16[1,896,1,256]{1,3,0,2:T(8,128)(2,1)}, bf16[1,896,1,256]{1,3,0,2:T(8,128)(2,1)S(1)}, u32[]{:S(2)}, u32[]{:S(2)}) collective-permute-start(bf16[1,896,1,256]{1,3,0,2:T(8,128)(2,1)} %get-tuple-element.19), channel_id=1, source_target_pairs={{0,1},{1,2},{2,3},{3,4},{4,5},{5,6},{6,7},{7,8},{8,9},{9,10},{10,1... | collective-permute-start | bytes 1376264 | tf_op jit(solution)/shard_map/ppermute | solution.py:52
  17.0 17.3 %collective-permute-start.1 = (bf16[1,896,1,256]{1,3,0,2:T(8,128)(2,1)}, bf16[1,896,1,256]{1,3,0,2:T(8,128)(2,1)S(1)}, u32[]{:S(2)}, u32[]{:S(2)}) collective-permute-start(bf16[1,896,1,256]{1,3,0,2:T(8,128)(2,1)} %get-tuple-element.18), channel_id=1, source_target_pairs={{0,2},{1,3},{2,4},{3,5},{4,6},{5,7},{6,8},{7,9},{8,10},{9,11},{10,... | collective-permute-start | bytes 1376264 | tf_op jit(solution)/shard_map/ppermute | solution.py:52
  19.6 24.7 %collective-permute-start.2 = (bf16[1,896,1,256]{1,3,0,2:T(8,128)(2,1)}, bf16[1,896,1,256]{1,3,0,2:T(8,128)(2,1)S(1)}, u32[]{:S(2)}, u32[]{:S(2)}) collective-permute-start(bf16[1,896,1,256]{1,3,0,2:T(8,128)(2,1)} %get-tuple-element.17), channel_id=1, source_target_pairs={{0,3},{1,4},{2,5},{3,6},{4,7},{5,8},{6,9},{7,10},{8,11},{9,12},{10... | collective-permute-start | bytes 1376264 | tf_op jit(solution)/shard_map/ppermute | solution.py:52
  22.0 24.8 %collective-permute-start.3 = (bf16[1,896,1,256]{1,3,0,2:T(8,128)(2,1)}, bf16[1,896,1,256]{1,3,0,2:T(8,128)(2,1)S(1)}, u32[]{:S(2)}, u32[]{:S(2)}) collective-permute-start(bf16[1,896,1,256]{1,3,0,2:T(8,128)(2,1)} %get-tuple-element.16), channel_id=1, source_target_pairs={{0,4},{1,5},{2,6},{3,7},{4,8},{5,9},{6,10},{7,11},{8,12},{9,13},{1... | collective-permute-start | bytes 1376264 | tf_op jit(solution)/shard_map/ppermute | solution.py:52
  23.6 88.3 %collective-permute-start.4 = (bf16[1,896,1,256]{1,3,0,2:T(8,128)(2,1)}, bf16[1,896,1,256]{1,3,0,2:T(8,128)(2,1)S(1)}, u32[]{:S(2)}, u32[]{:S(2)}) collective-permute-start(bf16[1,896,1,256]{1,3,0,2:T(8,128)(2,1)} %get-tuple-element.15), channel_id=1, source_target_pairs={{0,5},{1,6},{2,7},{3,8},{4,9},{5,10},{6,11},{7,12},{8,13},{9,14},{... | collective-permute-start | bytes 1376264 | tf_op jit(solution)/shard_map/ppermute | solution.py:52
  26.0 86.7 %copy-start.5 = (bf16[1,896,1,256]{1,3,0,2:T(8,128)(2,1)S(1)}, bf16[1,896,1,256]{1,3,0,2:T(8,128)(2,1)}, u32[]{:S(2)}) copy-start(bf16[1,896,1,256]{1,3,0,2:T(8,128)(2,1)} %get-tuple-element.9) | copy-start | bytes 1376260
  26.0 98.9 %copy-start.4 = (bf16[1,896,1,256]{1,3,0,2:T(8,128)(2,1)S(1)}, bf16[1,896,1,256]{1,3,0,2:T(8,128)(2,1)}, u32[]{:S(2)}) copy-start(bf16[1,896,1,256]{1,3,0,2:T(8,128)(2,1)} %get-tuple-element.8) | copy-start | bytes 1376260
  26.0 122.9 %copy-start.3 = (bf16[1,896,1,256]{1,3,0,2:T(8,128)(2,1)S(1)}, bf16[1,896,1,256]{1,3,0,2:T(8,128)(2,1)}, u32[]{:S(2)}) copy-start(bf16[1,896,1,256]{1,3,0,2:T(8,128)(2,1)} %get-tuple-element.7) | copy-start | bytes 1376260
  26.0 124.1 %copy-start.2 = (bf16[1,896,1,256]{1,3,0,2:T(8,128)(2,1)S(1)}, bf16[1,896,1,256]{1,3,0,2:T(8,128)(2,1)}, u32[]{:S(2)}) copy-start(bf16[1,896,1,256]{1,3,0,2:T(8,128)(2,1)} %get-tuple-element.6) | copy-start | bytes 1376260
  32.5 80.2 %collective-permute-start.5 = (bf16[1,896,1,256]{1,3,0,2:T(8,128)(2,1)}, bf16[1,896,1,256]{1,3,0,2:T(8,128)(2,1)S(1)}, u32[]{:S(2)}, u32[]{:S(2)}) collective-permute-start(bf16[1,896,1,256]{1,3,0,2:T(8,128)(2,1)} %get-tuple-element.14), channel_id=1, source_target_pairs={{0,6},{1,7},{2,8},{3,9},{4,10},{5,11},{6,12},{7,13},{8,14},{9,15},... | collective-permute-start | bytes 1376264 | tf_op jit(solution)/shard_map/ppermute | solution.py:52
  34.3 90.6 %collective-permute-start.6 = (bf16[1,896,1,256]{1,3,0,2:T(8,128)(2,1)}, bf16[1,896,1,256]{1,3,0,2:T(8,128)(2,1)S(1)}, u32[]{:S(2)}, u32[]{:S(2)}) collective-permute-start(bf16[1,896,1,256]{1,3,0,2:T(8,128)(2,1)} %get-tuple-element.13), channel_id=1, source_target_pairs={{0,7},{1,8},{2,9},{3,10},{4,11},{5,12},{6,13},{7,14},{8,15},{9,0},... | collective-permute-start | bytes 1376264 | tf_op jit(solution)/shard_map/ppermute | solution.py:52
  44.3 104.6 %collective-permute-start.7 = (bf16[1,896,1,256]{1,3,0,2:T(8,128)(2,1)}, bf16[1,896,1,256]{1,3,0,2:T(8,128)(2,1)S(1)}, u32[]{:S(2)}, u32[]{:S(2)}) collective-permute-start(bf16[1,896,1,256]{1,3,0,2:T(8,128)(2,1)} %get-tuple-element.12), channel_id=1, source_target_pairs={{0,8},{1,9},{2,10},{3,11},{4,12},{5,13},{6,14},{7,15},{8,0},{9,1},... | collective-permute-start | bytes 1376264 | tf_op jit(solution)/shard_map/ppermute | solution.py:52
  46.7 103.4 %collective-permute-start.8 = (bf16[1,896,1,256]{1,3,0,2:T(8,128)(2,1)}, bf16[1,896,1,256]{1,3,0,2:T(8,128)(2,1)S(1)}, u32[]{:S(2)}, u32[]{:S(2)}) collective-permute-start(bf16[1,896,1,256]{1,3,0,2:T(8,128)(2,1)} %get-tuple-element.11), channel_id=1, source_target_pairs={{0,9},{1,10},{2,11},{3,12},{4,13},{5,14},{6,15},{7,0},{8,1},{9,2},... | collective-permute-start | bytes 1376264 | tf_op jit(solution)/shard_map/ppermute | solution.py:52
  111.8 53.6 %collective-permute-start.9 = (bf16[1,896,1,256]{1,3,0,2:T(8,128)(2,1)}, bf16[1,896,1,256]{1,3,0,2:T(8,128)(2,1)S(1)}, u32[]{:S(2)}, u32[]{:S(2)}) collective-permute-start(bf16[1,896,1,256]{1,3,0,2:T(8,128)(2,1)} %get-tuple-element.10), channel_id=1, source_target_pairs={{0,10},{1,11},{2,12},{3,13},{4,14},{5,15},{6,0},{7,1},{8,2},{9,3},... | collective-permute-start | bytes 1376264 | tf_op jit(solution)/shard_map/ppermute | solution.py:52
  112.7 66.9 %collective-permute-start.10 = (bf16[1,896,1,256]{1,3,0,2:T(8,128)(2,1)S(1)}, bf16[1,896,1,256]{1,3,0,2:T(8,128)(2,1)S(1)}, u32[]{:S(2)}, u32[]{:S(2)}) collective-permute-start(bf16[1,896,1,256]{1,3,0,2:T(8,128)(2,1)S(1)} %copy-done.5), channel_id=1, source_target_pairs={{0,11},{1,12},{2,13},{3,14},{4,15},{5,0},{6,1},{7,2},{8,3},{9,4},{... | collective-permute-start | bytes 1376264 | tf_op jit(solution)/shard_map/ppermute | solution.py:52
  124.9 55.4 %collective-permute-start.11 = (bf16[1,896,1,256]{1,3,0,2:T(8,128)(2,1)S(1)}, bf16[1,896,1,256]{1,3,0,2:T(8,128)(2,1)S(1)}, u32[]{:S(2)}, u32[]{:S(2)}) collective-permute-start(bf16[1,896,1,256]{1,3,0,2:T(8,128)(2,1)S(1)} %copy-done.4), channel_id=1, source_target_pairs={{0,12},{1,13},{2,14},{3,15},{4,0},{5,1},{6,2},{7,3},{8,4},{9,5},{1... | collective-permute-start | bytes 1376264 | tf_op jit(solution)/shard_map/ppermute | solution.py:52
  148.9 32.3 %collective-permute-start.12 = (bf16[1,896,1,256]{1,3,0,2:T(8,128)(2,1)S(1)}, bf16[1,896,1,256]{1,3,0,2:T(8,128)(2,1)S(1)}, u32[]{:S(2)}, u32[]{:S(2)}) collective-permute-start(bf16[1,896,1,256]{1,3,0,2:T(8,128)(2,1)S(1)} %copy-done.3), channel_id=1, source_target_pairs={{0,13},{1,14},{2,15},{3,0},{4,1},{5,2},{6,3},{7,4},{8,5},{9,6},{10... | collective-permute-start | bytes 1376264 | tf_op jit(solution)/shard_map/ppermute | solution.py:52
  150.1 34.8 %collective-permute-start.13 = (bf16[1,896,1,256]{1,3,0,2:T(8,128)(2,1)S(1)}, bf16[1,896,1,256]{1,3,0,2:T(8,128)(2,1)S(1)}, u32[]{:S(2)}, u32[]{:S(2)}) collective-permute-start(bf16[1,896,1,256]{1,3,0,2:T(8,128)(2,1)S(1)} %copy-done.2), channel_id=1, source_target_pairs={{0,14},{1,15},{2,0},{3,1},{4,2},{5,3},{6,4},{7,5},{8,6},{9,7},{10,... | collective-permute-start | bytes 1376264 | tf_op jit(solution)/shard_map/ppermute | solution.py:52
  165.4 22.8 %collective-permute-start.14 = (bf16[1,896,1,256]{1,3,0,2:T(8,128)(2,1)S(1)}, bf16[1,896,1,256]{1,3,0,2:T(8,128)(2,1)S(1)}, u32[]{:S(2)}, u32[]{:S(2)}) collective-permute-start(bf16[1,896,1,256]{1,3,0,2:T(8,128)(2,1)S(1)} %get-tuple-element.5), channel_id=1, source_target_pairs={{0,15},{1,0},{2,1},{3,2},{4,3},{5,4},{6,5},{7,6},{8,7},{9,8},{10,9... | collective-permute-start | bytes 1376264 | tf_op jit(solution)/shard_map/ppermute | solution.py:52
  328.2 2.4 copy-start.1
  331.3 1.6 copy-start
